TPU v7x, 256 devices: a whole 4x4x8 slice. The times are simulated.
256 devices in a mesh: tm: 4 (over y), tile: 64 (over z, x, core).
Axes of the slice: x: 4, y: 4, z: 8, core: 2. Of those that a mesh axis runs over, the one named last changes fastest.
Arguments:
- states: float32 [4, 16, 256, 256], P('tm', None, 'tile'), may hold values from -6 to 6
- increments: float32 [4, 16, 256, 256], P('tm', None, 'tile'), may hold values from -6 to 6
- w_first: bfloat16 [9, 16, 128], replicated, may hold values from -0.5 to 0.5
- w_mid: bfloat16 [2, 9, 128, 128], replicated, may hold values from -0.1875 to 0.1875
- w_last: bfloat16 [9, 16, 128], replicated, may hold values from -0.1875 to 0.1875
- biases: float32 [3, 128], replicated, may hold values from -2 to 2
- cov_x: float32 [256, 256], replicated, may hold values from -4 to 24, as said below
- cov_y: float32 [256, 256], replicated, may hold values from -4 to 24, as said below
Outputs:
- multiplier: float32 [4, 16, 256, 256], P('tm', None, 'tile')
- update: float32 [4, 16, 256, 256], P('tm', None, 'tile')
Inputs may be any that keep to these rules, and one draw needn't show every extreme that they name: `cov_x`: symmetric positive definite. `cov_y`: symmetric positive definite.
All inputs are finite; a program needn't handle non-finite values.
Results may differ from a plain program's by a relative error of at most 0.0024.
Values may be sent and summed in bfloat16 or wider, within the bound.
A program may use at most 64 MiB of HBM per device.

v0:
```python
import jax
import jax.numpy as jnp
from jax import lax
from jax.sharding import PartitionSpec as P


def padded_2(block, sides, width):
    for axis, dim in sides:
        count = lax.axis_size(axis)
        forward = [(i, i + 1) for i in range(count - 1)]
        backward = [(target, source) for source, target in forward]
        low = lax.ppermute(
            lax.slice_in_dim(block, block.shape[dim] - width, None, axis=dim), axis, forward
        )
        high = lax.ppermute(lax.slice_in_dim(block, 0, width, axis=dim), axis, backward)
        block = jnp.concatenate([low, block, high], axis=dim)
    return block


def from_behind(block, axis, distance):
    devices = range(lax.axis_size(axis))
    route = [(i - distance, i) for i in devices if i - distance in devices]
    return lax.ppermute(block, axis, route)


def convolve(padded, kernel, pattern, flipped):
    height = padded.shape[2] - 2
    across = padded.shape[3]
    widened = jnp.pad(padded, ((0, 0), (0, 0), (0, 0), (1, 1)))
    summed = None
    for tap_index in range(9):
        row_off = tap_index // 3
        col_off = tap_index % 3
        if flipped:
            row_off = 2 - row_off
            col_off = 2 - col_off
        window = widened[:, :, row_off : row_off + height, col_off : col_off + across]
        contribution = jnp.einsum(
            pattern, kernel[tap_index], window, preferred_element_type=jnp.float32
        )
        summed = contribution if summed is None else summed + contribution
    return summed


def forward_rows(stacked):
    return padded_2(stacked, (("tile", 2),), 1)


def adjoint_rows(cotangent):
    return padded_2(cotangent, (("tile", 2),), 1)


def local(states, increments, w_first, w_mid, w_last, biases, cov_x, cov_y):
    windows_here = states.shape[0]
    height = states.shape[2]
    kernels = (w_first, w_mid[0], w_mid[1])
    current = jnp.concatenate((states, increments), axis=0).astype(jnp.bfloat16)
    slopes = []
    for layer_index in range(3):
        combined = convolve(forward_rows(current), kernels[layer_index], "co,scxy->soxy", False)
        primal = jnp.tanh(combined[:windows_here] + biases[layer_index][None, :, None, None])
        derivative = 1.0 - primal * primal
        slopes.append(derivative)
        tangent = (derivative * combined[windows_here:]).astype(jnp.bfloat16)
        if layer_index < 2:
            current = jnp.concatenate((primal.astype(jnp.bfloat16), tangent), axis=0)
        else:
            current = tangent
    change = convolve(forward_rows(current), w_last, "oc,scxy->soxy", False)
    following = from_behind(increments, "tm", -1)
    shifted_up = jnp.concatenate((increments[1:], following), axis=0)
    misfit = shifted_up - increments - change
    smoothed = jnp.einsum("sfxy,zy->sfxz", misfit, cov_y, precision=lax.Precision.HIGHEST)
    own_rows = lax.dynamic_slice_in_dim(cov_x, lax.axis_index("tile") * height, height, 0)
    multiplier = jnp.einsum(
        "ij,sfjz->sfiz",
        own_rows,
        lax.all_gather(smoothed, "tile", axis=2, tiled=True),
        precision=lax.Precision.HIGHEST,
    )
    cotangent = multiplier.astype(jnp.bfloat16)
    backward = convolve(adjoint_rows(cotangent), w_last, "oc,soxy->scxy", True)
    for layer_index in (2, 1, 0):
        cotangent = (slopes[layer_index] * backward).astype(jnp.bfloat16)
        backward = convolve(adjoint_rows(cotangent), kernels[layer_index], "co,soxy->scxy", True)
    earlier = from_behind(multiplier, "tm", 1)
    behind = jnp.concatenate((earlier, multiplier[:-1]), axis=0)
    update = behind - multiplier - backward
    return (multiplier, update)


def solution(mesh):
    in_specs = (
        P("tm", None, "tile", None),
        P("tm", None, "tile", None),
        P(),
        P(),
        P(),
        P(),
        P(),
        P(),
    )
    out_specs = (P("tm", None, "tile", None), P("tm", None, "tile", None))
    return jax.shard_map(local, mesh=mesh, in_specs=in_specs, out_specs=out_specs, check_vma=False)
```

profile of v0, /device:TPU:103, one launch (start us, length us, event | category | flops | bytes accessed | tf_op | source)
XLA Modules:
  0.0 214.0 jit_solution(12426863787796668289)
XLA Ops:
  9.0 5.2 %collective-permute-start.1 = (bf16[2,16,1,256]{3,1,2,0:T(8,128)(2,1)S(1)}, bf16[2,16,1,256]{3,1,2,0:T(8,128)(2,1)S(1)}, u32[]{:S(2)}, u32[]{:S(2)}) collective-permute-start(bf16[2,16,1,256]{3,1,2,0:T(8,128)(2,1)S(1)} %get-tuple-element.20), channel_id=1, source_target_pairs={{0,1},{1,2},{2,3},{3,4},{4,5},{5,6},{6,7},{7,8},{8,9},{9,10},{10,1... | collective-permute-start | bytes 49160 | tf_op jit(solution)/shard_map/ppermute | solution.py:12
  14.2 1.9 collective-permute-start.2
  17.0 5.6 %collective-permute-done.2 = bf16[2,16,1,256]{3,1,2,0:T(8,128)(2,1)S(1)} collective-permute-done((bf16[2,16,1,256]{3,1,2,0:T(8,128)(2,1)S(1)}, bf16[2,16,1,256]{3,1,2,0:T(8,128)(2,1)S(1)}, u32[]{:S(2)}, u32[]{:S(2)}) %collective-permute-start.2) | collective-permute-done | bytes 16416 | tf_op jit(solution)/shard_map/ppermute | solution.py:15
  27.1 1.9 collective-permute-start.3
  29.0 2.4 %collective-permute-start.4 = (bf16[2,128,1,256]{1,3,2,0:T(8,128)(2,1)S(1)}, bf16[2,128,1,256]{1,3,2,0:T(8,128)(2,1)S(1)}, u32[]{:S(2)}, u32[]{:S(2)}) collective-permute-start(bf16[2,128,1,256]{1,3,2,0:T(8,128)(2,1)S(1)} %get-tuple-element.11), channel_id=1, source_target_pairs={{1,0},{2,1},{3,2},{4,3},{5,4},{6,5},{7,6},{8,7},{9,8},{10,9},{11,1... | collective-permute-start | bytes 393224 | tf_op jit(solution)/shard_map/ppermute | solution.py:15
  31.4 7.2 %collective-permute-done.4 = bf16[2,128,1,256]{1,3,2,0:T(8,128)(2,1)S(1)} collective-permute-done((bf16[2,128,1,256]{1,3,2,0:T(8,128)(2,1)S(1)}, bf16[2,128,1,256]{1,3,2,0:T(8,128)(2,1)S(1)}, u32[]{:S(2)}, u32[]{:S(2)}) %collective-permute-start.4) | collective-permute-done | bytes 131104 | tf_op jit(solution)/shard_map/ppermute | solution.py:15
  41.6 1.9 collective-permute-start.5
  43.5 2.4 %collective-permute-start.6 = (bf16[2,128,1,256]{1,3,2,0:T(8,128)(2,1)S(1)}, bf16[2,128,1,256]{1,3,2,0:T(8,128)(2,1)S(1)}, u32[]{:S(2)}, u32[]{:S(2)}) collective-permute-start(bf16[2,128,1,256]{1,3,2,0:T(8,128)(2,1)S(1)} %get-tuple-element.9), channel_id=1, source_target_pairs={{1,0},{2,1},{3,2},{4,3},{5,4},{6,5},{7,6},{8,7},{9,8},{10,9},{11,1... | collective-permute-start | bytes 393224 | tf_op jit(solution)/shard_map/ppermute | solution.py:15
  46.0 7.2 %collective-permute-done.6 = bf16[2,128,1,256]{1,3,2,0:T(8,128)(2,1)S(1)} collective-permute-done((bf16[2,128,1,256]{1,3,2,0:T(8,128)(2,1)S(1)}, bf16[2,128,1,256]{1,3,2,0:T(8,128)(2,1)S(1)}, u32[]{:S(2)}, u32[]{:S(2)}) %collective-permute-start.6) | collective-permute-done | bytes 131104 | tf_op jit(solution)/shard_map/ppermute | solution.py:15
  56.2 1.9 collective-permute-start.7
  58.1 2.4 %collective-permute-start.8 = (bf16[1,128,1,256]{1,3,2,0:T(8,128)(2,1)S(1)}, bf16[1,128,1,256]{1,3,2,0:T(8,128)(2,1)S(1)}, u32[]{:S(2)}, u32[]{:S(2)}) collective-permute-start(bf16[1,128,1,256]{1,3,2,0:T(8,128)(2,1)S(1)} %get-tuple-element.19), channel_id=1, source_target_pairs={{1,0},{2,1},{3,2},{4,3},{5,4},{6,5},{7,6},{8,7},{9,8},{10,9},{11,1... | collective-permute-start | bytes 196616 | tf_op jit(solution)/shard_map/ppermute | solution.py:15
  62.1 5.0 %collective-permute-done.8 = bf16[1,128,1,256]{1,3,2,0:T(8,128)(2,1)S(1)} collective-permute-done((bf16[1,128,1,256]{1,3,2,0:T(8,128)(2,1)S(1)}, bf16[1,128,1,256]{1,3,2,0:T(8,128)(2,1)S(1)}, u32[]{:S(2)}, u32[]{:S(2)}) %collective-permute-start.8) | collective-permute-done | bytes 65568 | tf_op jit(solution)/shard_map/ppermute | solution.py:15
  69.9 75.9 %all-gather.3.cloned.1.call-done = f32[16,256,256]{2,0,1:T(8,128)} async-done(((f32[16,4,256]{2,0,1:T(8,128)}), f32[16,256,256]{2,0,1:T(8,128)}) %all-gather.3.cloned.1.call-update) | async-done | bytes 4194320 | tf_op jit(solution)/shard_map/all_gather | solution.py:78
  145.8 6.6 %fusion = f32[16,256,4]{1,2,0:T(4,128)S(1)} fusion(f32[16,256,256]{2,0,1:T(8,128)} %all-gather.3.cloned.1.call-done, f32[256,256]{1,0:T(8,128)} %param.14, s32[]{:T(128)S(6)} %select_n.3), kind=kOutput, calls=%fused_computation | convolution fusion | flops 50331648 | bytes 4263940 | tf_op jit(solution)/shard_map/ij,sfjz->sfiz/dot_general | solution.py:75
  152.4 4.0 %collective-permute-start.10 = (bf16[1,16,1,256]{3,1,2,0:T(8,128)(2,1)S(1)}, bf16[1,16,1,256]{3,1,2,0:T(8,128)(2,1)S(1)}, u32[]{:S(2)}, u32[]{:S(2)}) collective-permute-start(bf16[1,16,1,256]{3,1,2,0:T(8,128)(2,1)S(1)} %get-tuple-element.22), channel_id=1, source_target_pairs={{0,1},{1,2},{2,3},{3,4},{4,5},{5,6},{6,7},{7,8},{8,9},{9,10},{10,1... | collective-permute-start | bytes 24584 | tf_op jit(solution)/shard_map/ppermute | solution.py:12
  158.4 6.4 %collective-permute-done.11 = bf16[1,16,1,256]{3,1,2,0:T(8,128)(2,1)S(1)} collective-permute-done((bf16[1,16,1,256]{3,1,2,0:T(8,128)(2,1)S(1)}, bf16[1,16,1,256]{3,1,2,0:T(8,128)(2,1)S(1)}, u32[]{:S(2)}, u32[]{:S(2)}) %collective-permute-start.11) | collective-permute-done | bytes 8224 | tf_op jit(solution)/shard_map/ppermute | solution.py:15
  167.6 1.9 collective-permute-start.12
  169.5 2.4 %collective-permute-start.13 = (bf16[1,128,1,256]{1,3,2,0:T(8,128)(2,1)S(1)}, bf16[1,128,1,256]{1,3,2,0:T(8,128)(2,1)S(1)}, u32[]{:S(2)}, u32[]{:S(2)}) collective-permute-start(bf16[1,128,1,256]{1,3,2,0:T(8,128)(2,1)S(1)} %get-tuple-element.17), channel_id=1, source_target_pairs={{1,0},{2,1},{3,2},{4,3},{5,4},{6,5},{7,6},{8,7},{9,8},{10,9},{11,1... | collective-permute-start | bytes 196616 | tf_op jit(solution)/shard_map/ppermute | solution.py:15
  171.9 6.5 %collective-permute-done.13 = bf16[1,128,1,256]{1,3,2,0:T(8,128)(2,1)S(1)} collective-permute-done((bf16[1,128,1,256]{1,3,2,0:T(8,128)(2,1)S(1)}, bf16[1,128,1,256]{1,3,2,0:T(8,128)(2,1)S(1)}, u32[]{:S(2)}, u32[]{:S(2)}) %collective-permute-start.13) | collective-permute-done | bytes 65568 | tf_op jit(solution)/shard_map/ppermute | solution.py:15
  182.6 2.4 %collective-permute-start.15 = (bf16[1,128,1,256]{1,3,2,0:T(8,128)(2,1)S(1)}, bf16[1,128,1,256]{1,3,2,0:T(8,128)(2,1)S(1)}, u32[]{:S(2)}, u32[]{:S(2)}) collective-permute-start(bf16[1,128,1,256]{1,3,2,0:T(8,128)(2,1)S(1)} %get-tuple-element.15), channel_id=1, source_target_pairs={{1,0},{2,1},{3,2},{4,3},{5,4},{6,5},{7,6},{8,7},{9,8},{10,9},{11,1... | collective-permute-start | bytes 196616 | tf_op jit(solution)/shard_map/ppermute | solution.py:15
  185.1 6.5 %collective-permute-done.15 = bf16[1,128,1,256]{1,3,2,0:T(8,128)(2,1)S(1)} collective-permute-done((bf16[1,128,1,256]{1,3,2,0:T(8,128)(2,1)S(1)}, bf16[1,128,1,256]{1,3,2,0:T(8,128)(2,1)S(1)}, u32[]{:S(2)}, u32[]{:S(2)}) %collective-permute-start.15) | collective-permute-done | bytes 65568 | tf_op jit(solution)/shard_map/ppermute | solution.py:15
  195.8 2.4 %collective-permute-start.17 = (bf16[1,128,1,256]{1,3,2,0:T(8,128)(2,1)S(1)}, bf16[1,128,1,256]{1,3,2,0:T(8,128)(2,1)S(1)}, u32[]{:S(2)}, u32[]{:S(2)}) collective-permute-start(bf16[1,128,1,256]{1,3,2,0:T(8,128)(2,1)S(1)} %get-tuple-element.13), channel_id=1, source_target_pairs={{1,0},{2,1},{3,2},{4,3},{5,4},{6,5},{7,6},{8,7},{9,8},{10,9},{11,1... | collective-permute-start | bytes 196616 | tf_op jit(solution)/shard_map/ppermute | solution.py:15
  198.2 3.1 %collective-permute-start.9 = (f32[1,16,4,256]{3,1,2,0:T(8,128)S(1)}, f32[1,16,4,256]{3,1,2,0:T(8,128)S(1)}, u32[]{:S(2)}, u32[]{:S(2)}) collective-permute-start(f32[1,16,4,256]{3,1,2,0:T(8,128)S(1)} %bitcast.551), channel_id=1, source_target_pairs={{0,64},{64,128},{128,192},{1,65},{65,129},{129,193},{2,66},{66,130... | collective-permute-start | bytes 196616 | tf_op jit(solution)/shard_map/ppermute | solution.py:23
  202.0 2.7 %collective-permute-done.17 = bf16[1,128,1,256]{1,3,2,0:T(8,128)(2,1)S(1)} collective-permute-done((bf16[1,128,1,256]{1,3,2,0:T(8,128)(2,1)S(1)}, bf16[1,128,1,256]{1,3,2,0:T(8,128)(2,1)S(1)}, u32[]{:S(2)}, u32[]{:S(2)}) %collective-permute-start.17) | collective-permute-done | bytes 65568 | tf_op jit(solution)/shard_map/ppermute | solution.py:15
  (128 shorter events, 33.4 us)
Async XLA Ops:
  7.2 61.7 %copy-start = (f32[256,256]{1,0:T(8,128)S(1)}, f32[256,256]{1,0:T(8,128)}, u32[]{:S(2)}) copy-start(f32[256,256]{1,0:T(8,128)} %param.15) | copy-start | bytes 786436
  7.2 16.7 %copy-start.5 = (bf16[9,16,128]{2,1,0:T(8,128)(2,1)S(1)}, bf16[9,16,128]{2,1,0:T(8,128)(2,1)}, u32[]{:S(2)}) copy-start(bf16[9,16,128]{2,1,0:T(8,128)(2,1)} %param.10) | copy-start | bytes 110596
  7.2 138.6 %all-gather.3.cloned.1.call-start = ((), (), s32[]{:S(2)}) async-start(), calls=%async_computation | async-start | bytes 4259840 | tf_op jit(solution)/shard_map/all_gather | solution.py:78
  9.0 8.0 %collective-permute-start.1 = (bf16[2,16,1,256]{3,1,2,0:T(8,128)(2,1)S(1)}, bf16[2,16,1,256]{3,1,2,0:T(8,128)(2,1)S(1)}, u32[]{:S(2)}, u32[]{:S(2)}) collective-permute-start(bf16[2,16,1,256]{3,1,2,0:T(8,128)(2,1)S(1)} %get-tuple-element.20), channel_id=1, source_target_pairs={{0,1},{1,2},{2,3},{3,4},{4,5},{5,6},{6,7},{7,8},{8,9},{9,10},{10,1... | collective-permute-start | bytes 49160 | tf_op jit(solution)/shard_map/ppermute | solution.py:12
  14.2 8.4 %collective-permute-start.2 = (bf16[2,16,1,256]{3,1,2,0:T(8,128)(2,1)S(1)}, bf16[2,16,1,256]{3,1,2,0:T(8,128)(2,1)S(1)}, u32[]{:S(2)}, u32[]{:S(2)}) collective-permute-start(bf16[2,16,1,256]{3,1,2,0:T(8,128)(2,1)S(1)} %get-tuple-element.21), channel_id=1, source_target_pairs={{1,0},{2,1},{3,2},{4,3},{5,4},{6,5},{7,6},{8,7},{9,8},{10,9},{11,1... | collective-permute-start | bytes 49160 | tf_op jit(solution)/shard_map/ppermute | solution.py:15
  26.9 12.0 %copy-start.1 = (bf16[2,9,128,128]{3,2,1,0:T(8,128)(2,1)S(1)}, bf16[2,9,128,128]{3,2,1,0:T(8,128)(2,1)}, u32[]{:S(2)}) copy-start(bf16[2,9,128,128]{3,2,1,0:T(8,128)(2,1)} %param.11) | copy-start | bytes 1769476
  27.1 4.3 %collective-permute-start.3 = (bf16[2,128,1,256]{1,3,2,0:T(8,128)(2,1)S(1)}, bf16[2,128,1,256]{1,3,2,0:T(8,128)(2,1)S(1)}, u32[]{:S(2)}, u32[]{:S(2)}) collective-permute-start(bf16[2,128,1,256]{1,3,2,0:T(8,128)(2,1)S(1)} %get-tuple-element.10), channel_id=1, source_target_pairs={{0,1},{1,2},{2,3},{3,4},{4,5},{5,6},{6,7},{7,8},{8,9},{9,10},{10,1... | collective-permute-start | bytes 393224 | tf_op jit(solution)/shard_map/ppermute | solution.py:12
  29.0 9.6 %collective-permute-start.4 = (bf16[2,128,1,256]{1,3,2,0:T(8,128)(2,1)S(1)}, bf16[2,128,1,256]{1,3,2,0:T(8,128)(2,1)S(1)}, u32[]{:S(2)}, u32[]{:S(2)}) collective-permute-start(bf16[2,128,1,256]{1,3,2,0:T(8,128)(2,1)S(1)} %get-tuple-element.11), channel_id=1, source_target_pairs={{1,0},{2,1},{3,2},{4,3},{5,4},{6,5},{7,6},{8,7},{9,8},{10,9},{11,1... | collective-permute-start | bytes 393224 | tf_op jit(solution)/shard_map/ppermute | solution.py:15
  41.6 4.3 %collective-permute-start.5 = (bf16[2,128,1,256]{1,3,2,0:T(8,128)(2,1)S(1)}, bf16[2,128,1,256]{1,3,2,0:T(8,128)(2,1)S(1)}, u32[]{:S(2)}, u32[]{:S(2)}) collective-permute-start(bf16[2,128,1,256]{1,3,2,0:T(8,128)(2,1)S(1)} %get-tuple-element.8), channel_id=1, source_target_pairs={{0,1},{1,2},{2,3},{3,4},{4,5},{5,6},{6,7},{7,8},{8,9},{9,10},{10,1... | collective-permute-start | bytes 393224 | tf_op jit(solution)/shard_map/ppermute | solution.py:12
  43.5 9.6 %collective-permute-start.6 = (bf16[2,128,1,256]{1,3,2,0:T(8,128)(2,1)S(1)}, bf16[2,128,1,256]{1,3,2,0:T(8,128)(2,1)S(1)}, u32[]{:S(2)}, u32[]{:S(2)}) collective-permute-start(bf16[2,128,1,256]{1,3,2,0:T(8,128)(2,1)S(1)} %get-tuple-element.9), channel_id=1, source_target_pairs={{1,0},{2,1},{3,2},{4,3},{5,4},{6,5},{7,6},{8,7},{9,8},{10,9},{11,1... | collective-permute-start | bytes 393224 | tf_op jit(solution)/shard_map/ppermute | solution.py:15
  56.0 11.1 %copy-start.4 = (bf16[9,16,128]{2,1,0:T(8,128)(2,1)S(1)}, bf16[9,16,128]{2,1,0:T(8,128)(2,1)}, u32[]{:S(2)}) copy-start(bf16[9,16,128]{2,1,0:T(8,128)(2,1)} %param.12) | copy-start | bytes 110596
  56.2 5.9 %collective-permute-start.7 = (bf16[1,128,1,256]{1,3,2,0:T(8,128)(2,1)S(1)}, bf16[1,128,1,256]{1,3,2,0:T(8,128)(2,1)S(1)}, u32[]{:S(2)}, u32[]{:S(2)}) collective-permute-start(bf16[1,128,1,256]{1,3,2,0:T(8,128)(2,1)S(1)} %get-tuple-element.18), channel_id=1, source_target_pairs={{0,1},{1,2},{2,3},{3,4},{4,5},{5,6},{6,7},{7,8},{8,9},{9,10},{10,1... | collective-permute-start | bytes 196616 | tf_op jit(solution)/shard_map/ppermute | solution.py:12
  58.1 8.9 %collective-permute-start.8 = (bf16[1,128,1,256]{1,3,2,0:T(8,128)(2,1)S(1)}, bf16[1,128,1,256]{1,3,2,0:T(8,128)(2,1)S(1)}, u32[]{:S(2)}, u32[]{:S(2)}) collective-permute-start(bf16[1,128,1,256]{1,3,2,0:T(8,128)(2,1)S(1)} %get-tuple-element.19), channel_id=1, source_target_pairs={{1,0},{2,1},{3,2},{4,3},{5,4},{6,5},{7,6},{8,7},{9,8},{10,9},{11,1... | collective-permute-start | bytes 196616 | tf_op jit(solution)/shard_map/ppermute | solution.py:15
  60.6 8.3 %collective-permute-start = (f32[1,16,4,256]{3,1,2,0:T(8,128)S(1)}, f32[1,16,4,256]{3,1,2,0:T(8,128)S(1)}, u32[]{:S(2)}, u32[]{:S(2)}) collective-permute-start(f32[1,16,4,256]{3,1,2,0:T(8,128)S(1)} %copy.91), channel_id=1, source_target_pairs={{64,0},{128,64},{192,128},{65,1},{129,65},{193,129},{66,2},{130,66... | collective-permute-start | bytes 196616 | tf_op jit(solution)/shard_map/ppermute | solution.py:23
  152.4 6.0 %collective-permute-start.10 = (bf16[1,16,1,256]{3,1,2,0:T(8,128)(2,1)S(1)}, bf16[1,16,1,256]{3,1,2,0:T(8,128)(2,1)S(1)}, u32[]{:S(2)}, u32[]{:S(2)}) collective-permute-start(bf16[1,16,1,256]{3,1,2,0:T(8,128)(2,1)S(1)} %get-tuple-element.22), channel_id=1, source_target_pairs={{0,1},{1,2},{2,3},{3,4},{4,5},{5,6},{6,7},{7,8},{8,9},{9,10},{10,1... | collective-permute-start | bytes 24584 | tf_op jit(solution)/shard_map/ppermute | solution.py:12
  156.4 8.3 %collective-permute-start.11 = (bf16[1,16,1,256]{3,1,2,0:T(8,128)(2,1)S(1)}, bf16[1,16,1,256]{3,1,2,0:T(8,128)(2,1)S(1)}, u32[]{:S(2)}, u32[]{:S(2)}) collective-permute-start(bf16[1,16,1,256]{3,1,2,0:T(8,128)(2,1)S(1)} %get-tuple-element.23), channel_id=1, source_target_pairs={{1,0},{2,1},{3,2},{4,3},{5,4},{6,5},{7,6},{8,7},{9,8},{10,9},{11,1... | collective-permute-start | bytes 24584 | tf_op jit(solution)/shard_map/ppermute | solution.py:15
  167.2 11.3 %copy-start.2 = (bf16[2,9,128,128]{3,2,1,0:T(8,128)(2,1)S(1)}, bf16[2,9,128,128]{3,2,1,0:T(8,128)(2,1)}, u32[]{:S(2)}) copy-start(bf16[2,9,128,128]{3,2,1,0:T(8,128)(2,1)} %param.11) | copy-start | bytes 1769476
  167.6 4.3 %collective-permute-start.12 = (bf16[1,128,1,256]{1,3,2,0:T(8,128)(2,1)S(1)}, bf16[1,128,1,256]{1,3,2,0:T(8,128)(2,1)S(1)}, u32[]{:S(2)}, u32[]{:S(2)}) collective-permute-start(bf16[1,128,1,256]{1,3,2,0:T(8,128)(2,1)S(1)} %get-tuple-element.16), channel_id=1, source_target_pairs={{0,1},{1,2},{2,3},{3,4},{4,5},{5,6},{6,7},{7,8},{8,9},{9,10},{10,1... | collective-permute-start | bytes 196616 | tf_op jit(solution)/shard_map/ppermute | solution.py:12
  169.5 8.9 %collective-permute-start.13 = (bf16[1,128,1,256]{1,3,2,0:T(8,128)(2,1)S(1)}, bf16[1,128,1,256]{1,3,2,0:T(8,128)(2,1)S(1)}, u32[]{:S(2)}, u32[]{:S(2)}) collective-permute-start(bf16[1,128,1,256]{1,3,2,0:T(8,128)(2,1)S(1)} %get-tuple-element.17), channel_id=1, source_target_pairs={{1,0},{2,1},{3,2},{4,3},{5,4},{6,5},{7,6},{8,7},{9,8},{10,9},{11,1... | collective-permute-start | bytes 196616 | tf_op jit(solution)/shard_map/ppermute | solution.py:15
  180.7 4.3 %collective-permute-start.14 = (bf16[1,128,1,256]{1,3,2,0:T(8,128)(2,1)S(1)}, bf16[1,128,1,256]{1,3,2,0:T(8,128)(2,1)S(1)}, u32[]{:S(2)}, u32[]{:S(2)}) collective-permute-start(bf16[1,128,1,256]{1,3,2,0:T(8,128)(2,1)S(1)} %get-tuple-element.14), channel_id=1, source_target_pairs={{0,1},{1,2},{2,3},{3,4},{4,5},{5,6},{6,7},{7,8},{8,9},{9,10},{10,1... | collective-permute-start | bytes 196616 | tf_op jit(solution)/shard_map/ppermute | solution.py:12
  182.6 8.9 %collective-permute-start.15 = (bf16[1,128,1,256]{1,3,2,0:T(8,128)(2,1)S(1)}, bf16[1,128,1,256]{1,3,2,0:T(8,128)(2,1)S(1)}, u32[]{:S(2)}, u32[]{:S(2)}) collective-permute-start(bf16[1,128,1,256]{1,3,2,0:T(8,128)(2,1)S(1)} %get-tuple-element.15), channel_id=1, source_target_pairs={{1,0},{2,1},{3,2},{4,3},{5,4},{6,5},{7,6},{8,7},{9,8},{10,9},{11,1... | collective-permute-start | bytes 196616 | tf_op jit(solution)/shard_map/ppermute | solution.py:15
  193.9 8.2 %collective-permute-start.16 = (bf16[1,128,1,256]{1,3,2,0:T(8,128)(2,1)S(1)}, bf16[1,128,1,256]{1,3,2,0:T(8,128)(2,1)S(1)}, u32[]{:S(2)}, u32[]{:S(2)}) collective-permute-start(bf16[1,128,1,256]{1,3,2,0:T(8,128)(2,1)S(1)} %get-tuple-element.12), channel_id=1, source_target_pairs={{0,1},{1,2},{2,3},{3,4},{4,5},{5,6},{6,7},{7,8},{8,9},{9,10},{10,1... | collective-permute-start | bytes 196616 | tf_op jit(solution)/shard_map/ppermute | solution.py:12
  195.8 8.9 %collective-permute-start.17 = (bf16[1,128,1,256]{1,3,2,0:T(8,128)(2,1)S(1)}, bf16[1,128,1,256]{1,3,2,0:T(8,128)(2,1)S(1)}, u32[]{:S(2)}, u32[]{:S(2)}) collective-permute-start(bf16[1,128,1,256]{1,3,2,0:T(8,128)(2,1)S(1)} %get-tuple-element.13), channel_id=1, source_target_pairs={{1,0},{2,1},{3,2},{4,3},{5,4},{6,5},{7,6},{8,7},{9,8},{10,9},{11,1... | collective-permute-start | bytes 196616 | tf_op jit(solution)/shard_map/ppermute | solution.py:15
  198.2 8.1 %collective-permute-start.9 = (f32[1,16,4,256]{3,1,2,0:T(8,128)S(1)}, f32[1,16,4,256]{3,1,2,0:T(8,128)S(1)}, u32[]{:S(2)}, u32[]{:S(2)}) collective-permute-start(f32[1,16,4,256]{3,1,2,0:T(8,128)S(1)} %bitcast.551), channel_id=1, source_target_pairs={{0,64},{64,128},{128,192},{1,65},{65,129},{129,193},{2,66},{66,130... | collective-permute-start | bytes 196616 | tf_op jit(solution)/shard_map/ppermute | solution.py:23
  (1 other events, 4.5 us)
Sparse Core Ops, SparseCore 0:
  70.0 75.7 all-gather.2
where the time goes:
time: 215 us; the launch traced here: 214 us
  waiting for transfers between devices  123 us (57%)
  starting transfers between devices  43.7 us (20%)
  matrix products  27 us (13%)
  between operations  14.8 us (7%)
  local copies, waits for them, and re-layouts  4.05 us (2%)
    all_gather x1, waiting for transfers between devices, local(): lax.all_gather(smoothed, 'tile', axis=2, tiled=True)  75.9 us
    ppermute x8, waiting for transfers between devices, padded_2(): lax.ppermute(lax.slice_in_dim(block, 0, width, axis=dim), axis, backward)  47 us
    ppermute x8, starting transfers between devices, padded_2(): lax.ppermute(lax.slice_in_dim(block, block.shape[dim] - width, None, axis...  20.8 us
    dot_general x72, matrix products, convolve(): jnp.einsum(pattern, kernel[tap_index], window, preferred_element_type=jnp...  19.4 us
    ppermute x8, starting transfers between devices, padded_2(): lax.ppermute(lax.slice_in_dim(block, 0, width, axis=dim), axis, backward)  18.2 us
    dot_general x1, matrix products, local(): jnp.einsum('ij,sfjz->sfiz', own_rows, lax.all_gather(smoothed, 'tile', ax...  6.57 us
    ppermute x2, starting transfers between devices, from_behind(): return lax.ppermute(block, axis, route)  4.58 us
  transfers between devices with their start and end apart: 19, of which 9 were waited for; matrix products, arithmetic and copies ran while one was open for 2% of the time, Pallas kernels for 0%

commit v1 on v0

v1 whole, which is shorter than its diff:
```python
import jax
import jax.numpy as jnp
from jax import lax
from jax.experimental import pallas as pl
from jax.experimental.pallas import tpu as pltpu
from jax.sharding import PartitionSpec as P

F32 = jnp.float32
BF16 = jnp.bfloat16
MESH = pl.DeviceIdType.MESH
TILES = 64
WINDOWS = 4
CHIPS = 32


def contract(a, b, dims=((1,), (0,))):
    return lax.dot_general(a, b, (dims, ((), ())), preferred_element_type=F32)


def split(x):
    high = x.astype(BF16)
    return high, (x - high.astype(F32)).astype(BF16)


def shifted_rows(v):
    at = lax.broadcasted_iota(jnp.int32, (8, v.shape[1]), 0)
    up = pltpu.roll(v, 1, 0)
    down = pltpu.roll(v, v.shape[0] - 1, 0)
    up = jnp.concatenate([jnp.where(at == 0, 0.0, up[:8]), up[8:]], axis=0)
    down = jnp.concatenate([down[:-8], jnp.where(at == 7, 0.0, down[-8:])], axis=0)
    return up, down


def shifted_lanes(v):
    at = lax.broadcasted_iota(jnp.int32, v.shape, 1)
    n = v.shape[1]
    up = jnp.where(at == 0, 0.0, pltpu.roll(v, 1, 1))
    down = jnp.where(at == n - 1, 0.0, pltpu.roll(v, n - 1, 1))
    return up, down


def put_three(buf, i, v):
    up, down = shifted_rows(v)
    buf[i, :, 0:256] = up.astype(BF16)
    buf[i, :, 256:512] = v.astype(BF16)
    buf[i, :, 512:768] = down.astype(BF16)


def put_taps(buf, i, v):
    up, down = shifted_lanes(v)
    buf[i, 0:16] = up.astype(BF16)
    buf[i, 16:32] = v.astype(BF16)
    buf[i, 32:48] = down.astype(BF16)


def build_thin(dst, tap):
    zero = jnp.zeros((16, 128), BF16)
    for r in range(4):
        for q in range(3):
            for o in range(2):
                p = r - o
                at = (r * 3 + q) * 16
                block = tap(3 * p + q) if 0 <= p <= 2 else zero
                dst[at : at + 16, o * 128 : o * 128 + 128] = block


def build_wide(dst, tap):
    zero = jnp.zeros((128, 128), BF16)
    for pair in range(2):
        for q in range(3):
            for rr in range(2):
                for o in range(2):
                    p = 2 * pair + rr - o
                    at = pair * 768 + q * 256 + rr * 128
                    block = tap(3 * p + q) if 0 <= p <= 2 else zero
                    dst[at : at + 128, o * 128 : o * 128 + 128] = block


def wide_conv(buf, i, weights):
    both = jnp.concatenate([buf[i], buf[i + 1]], axis=1)
    return contract(both, weights[...])


def thin_conv(buf, i, weights):
    return contract(buf[i : i + 4].reshape(192, 256), weights[...], ((0,), (0,)))


def fold_rows(parts, r, flipped):
    sums = []
    for q in range(3):
        total = None
        for p in range(3):
            t = 3 * p + q
            t = 8 - t if flipped else t
            piece = parts[r + p][t * 16 : t * 16 + 16]
            total = piece if total is None else total + piece
        sums.append(total)
    up, _ = shifted_lanes(sums[0])
    _, down = shifted_lanes(sums[2])
    return up + sums[1] + down


def kernel(
    st, inc, wf_h, wm_h, wl_h, bias, cx_h, cy_h,
    mult_o, upd_o,
    wf, wm, wl, cx, cy,
    x, xq, tq, a1, t1, a2, t2, t3, b3, b2, b1, s1, s2, s3,
    w1, wk2, wk3, v4, vk3, vk2, cx3, cy3,
    nxt, prev, chg, sbuf, rbuf, obuf, mbuf,
    wsem, hs, hr, ns, nr, ps, pr, as_, ar, at_s, at_r, al, bs, br, bt_s, bt_r, bl,
):
    tm = lax.axis_index("tm")
    me = lax.axis_index("tile")
    chip = lax.div(me, 2)
    core = lax.rem(me, 2)
    tm_next = lax.rem(tm + 1, WINDOWS)
    tm_back = lax.rem(tm + WINDOWS - 1, WINDOWS)

    barrier = pltpu.get_barrier_semaphore()

    def greet(i, carry):
        to = lax.rem(me + i, TILES)
        pl.semaphore_signal(barrier, inc=1, device_id={"tile": to}, device_id_type=MESH)
        return carry

    lax.fori_loop(1, TILES, greet, 0)
    for to in (tm_next, tm_back):
        pl.semaphore_signal(barrier, inc=1, device_id={"tm": to}, device_id_type=MESH)

    loads = [
        pltpu.make_async_copy(src, dst, wsem.at[n])
        for n, (src, dst) in enumerate(
            ((wf_h, wf), (wm_h, wm), (wl_h, wl), (cx_h, cx), (cy_h, cy))
        )
    ]
    for load in loads:
        load.start()

    for r in range(4):
        x[6 + r, 0] = st[0, :, r, :].astype(BF16)
        x[6 + r, 1] = inc[0, :, r, :].astype(BF16)

    pl.semaphore_wait(barrier, TILES - 1 + 2)

    halo = []
    for n, (step, src, dst) in enumerate(
        (
            (1, x.at[6:10], x.at[2:6]),
            (TILES - 1, x.at[6:10], x.at[10:14]),
            (2, x.at[8:10, 0], x.at[0:2, 0]),
            (TILES - 2, x.at[6:8, 0], x.at[14:16, 0]),
        )
    ):
        halo.append(
            pltpu.make_async_remote_copy(
                src, dst, hs.at[n], hr.at[n],
                device_id={"tile": lax.rem(me + step, TILES)}, device_id_type=MESH,
            )
        )
    for copy in halo:
        copy.start()
    ahead = pltpu.make_async_remote_copy(
        inc.at[0], nxt, ns, nr, device_id={"tm": tm_back}, device_id_type=MESH
    )
    ahead.start()

    def valid(e):
        g = 4 * me - 6 + e
        return jnp.where((g >= 0) & (g < 4 * TILES), 1.0, 0.0).astype(F32)

    def pair_mask(e):
        lane = lax.broadcasted_iota(jnp.int32, (1, 256), 1)
        return jnp.where(lane < 128, valid(e), valid(e + 1))

    def inner(e):
        return e >= 6 and e + 1 <= 9

    for e in range(6, 10):
        put_taps(xq, e, x[e, 0].astype(F32))
        put_taps(tq, e, x[e, 1].astype(F32))
    loads[0].wait()
    build_thin(w1, lambda t: wf[t])
    loads[1].wait()
    build_wide(wk2, lambda t: wm[0, t])
    build_wide(wk3, lambda t: wm[1, t])
    loads[2].wait()
    build_thin(v4, lambda t: wl[8 - t])
    loads[3].wait()
    high, low = split(cx[...])
    cx3[:, 0:256] = high
    cx3[:, 256:512] = high
    cx3[:, 512:768] = low
    loads[4].wait()
    high, low = split(cy[...])
    cy3[0:256] = high
    cy3[256:512] = high
    cy3[512:768] = low
    biases = [jnp.concatenate([bias[l : l + 1], bias[l : l + 1]], axis=1) for l in range(3)]

    for copy in halo[:2]:
        copy.wait_recv()

    def edge_row(e, with_tangent):
        put_taps(xq, e, x[e, 0].astype(F32) * valid(e))
        if with_tangent:
            put_taps(tq, e, x[e, 1].astype(F32) * valid(e))

    for e in (2, 3, 4, 5, 10, 11, 12, 13):
        edge_row(e, True)

    def activation(l, z, e, s_buf, i, out):
        h = jnp.tanh(z + biases[l])
        s = 1.0 - h * h
        if not inner(e):
            mask = pair_mask(e)
            s = s * mask
            h = h * mask
        s_buf[i] = s
        if out is not None:
            put_three(out, i, h)
        return s

    def layer_one(i, tangent):
        s = activation(0, thin_conv(xq, 2 * i, w1), 2 * i + 1, s1, i, a1)
        if tangent:
            put_three(t1, i, s * thin_conv(tq, 2 * i, w1))

    def layer_two(i, tangent):
        s = activation(1, wide_conv(a1, i, wk2), 2 * i + 2, s2, i, a2)
        if tangent:
            put_three(t2, i, s * wide_conv(t1, i, wk2))

    def layer_three(i, tangent):
        s = activation(2, wide_conv(a2, i, wk3), 2 * i + 3, s3, i, None)
        if tangent:
            t3[i] = (s * wide_conv(t2, i, wk3)).astype(BF16)

    for i in range(1, 6):
        layer_one(i, True)
    for i in range(1, 5):
        layer_two(i, True)
    for i in range(1, 4):
        layer_three(i, True)

    last = wl[...].reshape(144, 128)
    parts = []
    for i in range(1, 4):
        for half in range(2):
            parts.append(contract(last, t3[i, :, half * 128 : half * 128 + 128], ((1,), (1,))))
    for r in range(4):
        chg[:, r, :] = fold_rows(parts, r, False)

    ahead.wait_recv()
    not_last = jnp.where(tm == WINDOWS - 1, 0.0, 1.0).astype(F32)
    misfit = nxt[...] * not_last - inc[0] - chg[...]
    high, low = split(misfit.reshape(64, 256))
    smoothed = contract(jnp.concatenate([high, low, high], axis=1), cy3[...])
    for half in range(2):
        sbuf[half * 16 : half * 16 + 16] = smoothed[:, half * 128 : half * 128 + 128].reshape(
            16, 4, 128
        )

    def out_chunk(i, send, recv):
        c = lax.rem(chip + i, CHIPS)
        return pltpu.make_async_remote_copy(
            sbuf.at[c], rbuf.at[me], send, recv,
            device_id={"tile": 2 * c}, device_id_type=MESH,
        )

    def start_chunk(i, carry):
        out_chunk(i, as_, ar).start()
        return carry

    lax.fori_loop(1, CHIPS, start_chunk, 0)
    own_chunk = pltpu.make_async_copy(sbuf.at[chip], rbuf.at[me], al)

    @pl.when(core == 0)
    def _():
        own_chunk.start()

    @pl.when(core == 1)
    def _():
        out_chunk(0, at_s, at_r).start()

    for copy in halo[2:]:
        copy.wait_recv()
    for e in (0, 1, 14, 15):
        edge_row(e, False)
    for i in (0, 6):
        layer_one(i, False)
    for i in (0, 5):
        layer_two(i, False)
    for i in (0, 4):
        layer_three(i, False)
    build_wide(vk3, lambda t: wm[1, 8 - t].T)
    build_wide(vk2, lambda t: wm[0, 8 - t].T)

    @pl.when(core == 0)
    def _():
        obuf[0] = jnp.zeros((4, 128), F32)
        obuf[TILES + 1] = jnp.zeros((4, 128), F32)
        own_chunk.wait()
        partner = pltpu.make_async_remote_copy(
            sbuf.at[0], rbuf.at[me + 1], at_s, at_r,
            device_id={"tile": me}, device_id_type=MESH,
        )
        partner.wait_recv()
        pltpu.make_async_copy(
            rbuf.at[0 : TILES - 2], rbuf.at[0 : TILES - 2], ar
        ).wait()
        high, low = split(rbuf[...].reshape(256, 128))
        result = contract(cx3[...], jnp.concatenate([high, low, high], axis=0))
        obuf[1 : TILES + 1] = result.reshape(TILES, 4, 128)

        def back_chunk(d, send, recv):
            return pltpu.make_async_remote_copy(
                obuf.at[pl.ds(d, 3)], mbuf.at[chip], send, recv,
                device_id={"tile": d}, device_id_type=MESH,
            )

        def start_back(i, carry):
            back_chunk(lax.rem(me + i, TILES), bs, br).start()
            return carry

        lax.fori_loop(2, TILES, start_back, 0)
        back_chunk(me + 1, bt_s, bt_r).start()
        own_back = pltpu.make_async_copy(obuf.at[pl.ds(me, 3)], mbuf.at[chip], bl)
        own_back.start()
        own_back.wait()

    @pl.when(core == 1)
    def _():
        pltpu.make_async_remote_copy(
            obuf.at[0:3], mbuf.at[chip], bt_s, bt_r,
            device_id={"tile": me}, device_id_type=MESH,
        ).wait_recv()

    pltpu.make_async_copy(mbuf.at[0 : CHIPS - 1], mbuf.at[0 : CHIPS - 1], br).wait()

    behind = pltpu.make_async_remote_copy(
        mbuf.at[:, 1], prev, ps, pr, device_id={"tm": tm_next}, device_id_type=MESH
    )
    behind.start()

    for idx in range(12):
        j, k = idx // 4, idx % 4
        row = jnp.concatenate([mbuf[0:16, j, k, :], mbuf[16:32, j, k, :]], axis=1)
        if j != 1:
            row = row * valid(2 + idx)
        put_taps(xq, idx, row.astype(BF16).astype(F32))
    for i in range(5):
        b = s3[i] * thin_conv(xq, 2 * i, v4)
        put_three(b3, i, b)
    for i in range(4):
        put_three(b2, i, s2[i + 1] * wide_conv(b3, i, vk3))
    for i in range(3):
        b1[i] = (s1[i + 2] * wide_conv(b2, i, vk2)).astype(BF16)
    first = wf[...].reshape(144, 128)
    parts = []
    for i in range(3):
        for half in range(2):
            parts.append(contract(first, b1[i, :, half * 128 : half * 128 + 128], ((1,), (1,))))
    for r in range(4):
        chg[:, r, :] = fold_rows(parts, r, True)

    behind.wait_recv()
    not_first = jnp.where(tm == 0, 0.0, 1.0).astype(F32)
    for half in range(2):
        lanes = slice(half * 128, half * 128 + 128)
        chunk = slice(half * 16, half * 16 + 16)
        own = mbuf[chunk, 1]
        mult_o[0, :, :, lanes] = own
        upd_o[0, :, :, lanes] = prev[chunk] * not_first - own - chg[:, :, lanes]

    for copy in halo:
        copy.wait_send()
    ahead.wait_send()
    behind.wait_send()
    pltpu.make_async_copy(sbuf.at[0 : CHIPS - 1], sbuf.at[0 : CHIPS - 1], as_).wait()

    @pl.when(core == 1)
    def _():
        pltpu.make_async_copy(sbuf.at[0], sbuf.at[0], at_s).wait()

    @pl.when(core == 0)
    def _():
        pltpu.make_async_copy(obuf.at[0:3], obuf.at[0:3], bt_s).wait()
        sent = mbuf.at[0 : CHIPS - 1]
        pltpu.make_async_copy(sent, sent, bs).wait()
        pltpu.make_async_copy(sent, sent, bs).wait()


def local(states, increments, w_first, w_mid, w_last, biases, cov_x, cov_y):
    vmem = pl.BlockSpec(memory_space=pltpu.VMEM)
    anywhere = pl.BlockSpec(memory_space=pl.ANY)
    dma = pltpu.SemaphoreType.DMA
    scratch = [
        pltpu.VMEM((9, 16, 128), BF16),
        pltpu.VMEM((2, 9, 128, 128), BF16),
        pltpu.VMEM((9, 16, 128), BF16),
        pltpu.VMEM((256, 256), F32),
        pltpu.VMEM((256, 256), F32),
        pltpu.VMEM((16, 2, 16, 256), BF16),
        pltpu.VMEM((16, 48, 256), BF16),
        pltpu.VMEM((16, 48, 256), BF16),
        pltpu.VMEM((7, 256, 768), BF16),
        pltpu.VMEM((7, 256, 768), BF16),
        pltpu.VMEM((6, 256, 768), BF16),
        pltpu.VMEM((6, 256, 768), BF16),
        pltpu.VMEM((5, 256, 256), BF16),
        pltpu.VMEM((5, 256, 768), BF16),
        pltpu.VMEM((4, 256, 768), BF16),
        pltpu.VMEM((3, 256, 256), BF16),
        pltpu.VMEM((7, 256, 256), F32),
        pltpu.VMEM((6, 256, 256), F32),
        pltpu.VMEM((5, 256, 256), F32),
        pltpu.VMEM((192, 256), BF16),
        pltpu.VMEM((1536, 256), BF16),
        pltpu.VMEM((1536, 256), BF16),
        pltpu.VMEM((192, 256), BF16),
        pltpu.VMEM((1536, 256), BF16),
        pltpu.VMEM((1536, 256), BF16),
        pltpu.VMEM((256, 768), BF16),
        pltpu.VMEM((768, 256), BF16),
        pltpu.VMEM((16, 4, 256), F32),
        pltpu.VMEM((32, 4, 128), F32),
        pltpu.VMEM((16, 4, 256), F32),
        pltpu.VMEM((32, 4, 128), F32),
        pltpu.VMEM((TILES, 4, 128), F32),
        pltpu.VMEM((TILES + 2, 4, 128), F32),
        pltpu.VMEM((32, 3, 4, 128), F32),
        dma((5,)), dma((4,)), dma((4,)),
        dma, dma, dma, dma,
        dma, dma, dma, dma, dma,
        dma, dma, dma, dma, dma,
    ]
    return pl.pallas_call(
        kernel,
        out_shape=[
            jax.ShapeDtypeStruct(states.shape, F32),
            jax.ShapeDtypeStruct(states.shape, F32),
        ],
        in_specs=[vmem, vmem, anywhere, anywhere, anywhere, vmem, anywhere, anywhere],
        out_specs=[vmem, vmem],
        scratch_shapes=scratch,
        compiler_params=pltpu.CompilerParams(collective_id=0, has_side_effects=True),
    )(states, increments, w_first, w_mid, w_last, biases, cov_x, cov_y)


def solution(mesh):
    block = P("tm", None, "tile", None)
    return jax.shard_map(
        local,
        mesh=mesh,
        in_specs=(block, block, P(), P(), P(), P(), P(), P()),
        out_specs=(block, block),
        check_vma=False,
    )
```

time: 215 us -> 43.5 us (0.20)
  the two profiles are of different devices: /device:TPU:103 before, /device:TPU:1 now
where the time goes in v1:
time: 43.5 us; the launch traced here: 43.3 us
  Pallas kernels  40.5 us (93%)
  local copies, waits for them, and re-layouts  2.14 us (5%)
  between operations  0.65 us (1%)
    pallas_call x1, Pallas kernels, local(): pl.pallas_call(kernel, out_shape=[jax.ShapeDtypeStruct(states.shape, F32)...  40.5 us
    unnamed x4, local copies, waits for them, and re-layouts  2.14 us

profile of v1, /device:TPU:1, one launch (start us, length us, event | category | flops | bytes accessed | tf_op | source)
XLA Modules:
  0.0 43.3 jit_solution(7978395390405435980)
XLA Ops:
  0.6 40.5 %shard_map.95 = (f32[1,16,4,256]{3,2,1,0:T(4,128)}, f32[1,16,4,256]{3,2,1,0:T(4,128)}) custom-call(f32[1,16,4,256]{3,2,1,0:T(4,128)} %st.1, f32[1,16,4,256]{3,2,1,0:T(4,128)} %inc.1, bf16[9,16,128]{2,1,0:T(8,128)(2,1)} %wf_h.1, bf16[2,9,128,128]{3,2,1,0:T(8,128)(2,1)} %wm_h.1, bf16[9,16,128]{2,1,0:T(8,128)(2,1)} %wl_h.1, f32[3,128]{1,0:T(4,128)} %bias.1, ...), custom_call_target="tpu_custom_call" | custom-call | tf_op jit(solution)/shard_map/pallas_call | solution.py:437
  41.2 0.0 copy-start
  41.2 1.5 %copy.12 = f32[1,16,4,256]{3,2,1,0:T(4,128)} copy(f32[1,16,4,256]{3,2,1,0:T(4,128)} %get-tuple-element.4) | data formatting | bytes 131072
  42.7 0.0 copy-done
  42.7 0.6 %copy.13 = f32[1,16,4,256]{3,2,1,0:T(4,128)} copy(f32[1,16,4,256]{3,2,1,0:T(4,128)S(1)} %copy-done) | data formatting | bytes 131072
Async XLA Ops:
  41.2 1.5 %copy-start = (f32[1,16,4,256]{3,2,1,0:T(4,128)S(1)}, f32[1,16,4,256]{3,2,1,0:T(4,128)}, u32[]{:S(2)}) copy-start(f32[1,16,4,256]{3,2,1,0:T(4,128)} %get-tuple-element.5) | copy-start | bytes 196612

commit v2 on v1

--- a/solution.py
+++ b/solution.py
@@ -11,6 +11,10 @@
 TILES = 64
 WINDOWS = 4
 CHIPS = 32
+FAR_FIRST = sorted(
+    ((z, x) for z in range(8) for x in range(4) if z or x),
+    key=lambda s: -(min(s[0], 8 - s[0]) + min(s[1], 4 - s[1])),
+)
 
 
 def contract(a, b, dims=((1,), (0,))):
@@ -101,13 +105,13 @@
 
 
 def kernel(
-    st, inc, wf_h, wm_h, wl_h, bias, cx_h, cy_h,
-    mult_o, upd_o,
-    wf, wm, wl, cx, cy,
+    st_h, inc_h, wf_h, wm_h, wl_h, bias_h, cx_h, cy_h,
+    high_o, low_o, rest_o,
+    st, inc, bias, wf, wm, wl, cx, cy,
     x, xq, tq, a1, t1, a2, t2, t3, b3, b2, b1, s1, s2, s3,
     w1, wk2, wk3, v4, vk3, vk2, cx3, cy3,
-    nxt, prev, chg, sbuf, rbuf, obuf, mbuf,
-    wsem, hs, hr, ns, nr, ps, pr, as_, ar, at_s, at_r, al, bs, br, bt_s, bt_r, bl,
+    nxt, prev, chg, bx, sbuf, rbuf, obuf, mbuf, high_v, low_v, rest_v,
+    insem, wsem, outsem, near, hs, hr, ns, nr, ps, pr, as_, ar, at_s, at_r, al, bs, br, bt_s, bt_r, bl,
 ):
     tm = lax.axis_index("tm")
     me = lax.axis_index("tile")
@@ -116,31 +120,47 @@
     tm_next = lax.rem(tm + 1, WINDOWS)
     tm_back = lax.rem(tm + WINDOWS - 1, WINDOWS)
 
+    def tile_at(step):
+        return lax.rem(me + (step + TILES), TILES)
+
     barrier = pltpu.get_barrier_semaphore()
-
-    def greet(i, carry):
-        to = lax.rem(me + i, TILES)
-        pl.semaphore_signal(barrier, inc=1, device_id={"tile": to}, device_id_type=MESH)
-        return carry
-
-    lax.fori_loop(1, TILES, greet, 0)
+    for step in (1, -1, 2, -2):
+        pl.semaphore_signal(
+            barrier, inc=1, device_id={"tile": tile_at(step)}, device_id_type=MESH
+        )
     for to in (tm_next, tm_back):
         pl.semaphore_signal(barrier, inc=1, device_id={"tm": to}, device_id_type=MESH)
 
+    takes = [
+        pltpu.make_async_copy(src, dst, insem.at[n])
+        for n, (src, dst) in enumerate(((st_h, st), (inc_h, inc), (bias_h, bias)))
+    ]
     loads = [
         pltpu.make_async_copy(src, dst, wsem.at[n])
         for n, (src, dst) in enumerate(
             ((wf_h, wf), (wm_h, wm), (wl_h, wl), (cx_h, cx), (cy_h, cy))
         )
     ]
-    for load in loads:
+    for load in takes + loads:
         load.start()
 
+    def tell(n):
+        for step in (2 << n, -(2 << n)):
+            pl.semaphore_signal(
+                near.at[n], inc=1, device_id={"tile": tile_at(step)}, device_id_type=MESH
+            )
+
+    def hear(n):
+        pl.semaphore_wait(near.at[n], 2)
+
+    takes[0].wait()
     for r in range(4):
         x[6 + r, 0] = st[0, :, r, :].astype(BF16)
+    takes[1].wait()
+    for r in range(4):
         x[6 + r, 1] = inc[0, :, r, :].astype(BF16)
 
-    pl.semaphore_wait(barrier, TILES - 1 + 2)
+    pl.semaphore_wait(barrier, 6)
 
     halo = []
     for n, (step, src, dst) in enumerate(
@@ -163,6 +183,7 @@
         inc.at[0], nxt, ns, nr, device_id={"tm": tm_back}, device_id_type=MESH
     )
     ahead.start()
+    tell(0)
 
     def valid(e):
         g = 4 * me - 6 + e
@@ -195,8 +216,11 @@
     cy3[0:256] = high
     cy3[256:512] = high
     cy3[512:768] = low
+    takes[2].wait()
     biases = [jnp.concatenate([bias[l : l + 1], bias[l : l + 1]], axis=1) for l in range(3)]
 
+    hear(0)
+    tell(1)
     for copy in halo[:2]:
         copy.wait_recv()
 
@@ -237,8 +261,12 @@
 
     for i in range(1, 6):
         layer_one(i, True)
+    hear(1)
+    tell(2)
     for i in range(1, 5):
         layer_two(i, True)
+    hear(2)
+    tell(3)
     for i in range(1, 4):
         layer_three(i, True)
 
@@ -260,18 +288,19 @@
             16, 4, 128
         )
 
-    def out_chunk(i, send, recv):
-        c = lax.rem(chip + i, CHIPS)
+    hear(3)
+
+    def chip_at(dz, dx):
+        return lax.rem(lax.div(chip, 4) + dz, 8) * 4 + lax.rem(chip + dx, 4)
+
+    def out_chunk(c, send, recv):
         return pltpu.make_async_remote_copy(
             sbuf.at[c], rbuf.at[me], send, recv,
             device_id={"tile": 2 * c}, device_id_type=MESH,
         )
 
-    def start_chunk(i, carry):
-        out_chunk(i, as_, ar).start()
-        return carry
-
-    lax.fori_loop(1, CHIPS, start_chunk, 0)
+    for dz, dx in FAR_FIRST:
+        out_chunk(chip_at(dz, dx), as_, ar).start()
     own_chunk = pltpu.make_async_copy(sbuf.at[chip], rbuf.at[me], al)
 
     @pl.when(core == 0)
@@ -280,7 +309,7 @@
 
     @pl.when(core == 1)
     def _():
-        out_chunk(0, at_s, at_r).start()
+        out_chunk(chip, at_s, at_r).start()
 
     for copy in halo[2:]:
         copy.wait_recv()
@@ -297,8 +326,8 @@
 
     @pl.when(core == 0)
     def _():
-        obuf[0] = jnp.zeros((4, 128), F32)
-        obuf[TILES + 1] = jnp.zeros((4, 128), F32)
+        obuf[0, 0] = jnp.zeros((4, 128), BF16)
+        obuf[TILES - 1, 1] = jnp.zeros((4, 128), BF16)
         own_chunk.wait()
         partner = pltpu.make_async_remote_copy(
             sbuf.at[0], rbuf.at[me + 1], at_s, at_r,
@@ -310,44 +339,62 @@
         ).wait()
         high, low = split(rbuf[...].reshape(256, 128))
         result = contract(cx3[...], jnp.concatenate([high, low, high], axis=0))
-        obuf[1 : TILES + 1] = result.reshape(TILES, 4, 128)
+        high, low = split(result)
+        high = high.reshape(TILES, 4, 128)
+        obuf[1:TILES, 0] = high[0 : TILES - 1]
+        obuf[0 : TILES - 1, 1] = high[1:TILES]
+        obuf[:, 2] = high
+        obuf[:, 3] = low.reshape(TILES, 4, 128)
 
         def back_chunk(d, send, recv):
             return pltpu.make_async_remote_copy(
-                obuf.at[pl.ds(d, 3)], mbuf.at[chip], send, recv,
+                obuf.at[d], mbuf.at[chip], send, recv,
                 device_id={"tile": d}, device_id_type=MESH,
             )
 
-        def start_back(i, carry):
-            back_chunk(lax.rem(me + i, TILES), bs, br).start()
-            return carry
-
-        lax.fori_loop(2, TILES, start_back, 0)
+        for dz, dx in FAR_FIRST:
+            c = chip_at(dz, dx)
+            for half in range(2):
+                back_chunk(2 * c + half, bs, br).start()
         back_chunk(me + 1, bt_s, bt_r).start()
-        own_back = pltpu.make_async_copy(obuf.at[pl.ds(me, 3)], mbuf.at[chip], bl)
+        own_back = pltpu.make_async_copy(obuf.at[me], mbuf.at[chip], bl)
         own_back.start()
         own_back.wait()
 
     @pl.when(core == 1)
     def _():
         pltpu.make_async_remote_copy(
-            obuf.at[0:3], mbuf.at[chip], bt_s, bt_r,
+            obuf.at[0], mbuf.at[chip], bt_s, bt_r,
             device_id={"tile": me}, device_id_type=MESH,
         ).wait_recv()
 
     pltpu.make_async_copy(mbuf.at[0 : CHIPS - 1], mbuf.at[0 : CHIPS - 1], br).wait()
 
     behind = pltpu.make_async_remote_copy(
-        mbuf.at[:, 1], prev, ps, pr, device_id={"tm": tm_next}, device_id_type=MESH
+        mbuf.at[:, 2:4], prev, ps, pr, device_id={"tm": tm_next}, device_id_type=MESH
     )
     behind.start()
 
+    for half in range(2):
+        lanes = slice(half * 128, half * 128 + 128)
+        chunk = slice(half * 16, half * 16 + 16)
+        for j, slot in enumerate((0, 2, 1)):
+            bx[j, :, :, lanes] = mbuf[chunk, slot].astype(F32)
+        high_v[0, :, :, lanes] = mbuf[chunk, 2]
+        low_v[0, :, :, lanes] = mbuf[chunk, 3]
+    outs = [
+        pltpu.make_async_copy(src, dst, outsem.at[n])
+        for n, (src, dst) in enumerate(((high_v, high_o), (low_v, low_o), (rest_v, rest_o)))
+    ]
+    outs[0].start()
+    outs[1].start()
+
     for idx in range(12):
         j, k = idx // 4, idx % 4
-        row = jnp.concatenate([mbuf[0:16, j, k, :], mbuf[16:32, j, k, :]], axis=1)
+        row = bx[j, :, k, :]
         if j != 1:
             row = row * valid(2 + idx)
-        put_taps(xq, idx, row.astype(BF16).astype(F32))
+        put_taps(xq, idx, row)
     for i in range(5):
         b = s3[i] * thin_conv(xq, 2 * i, v4)
         put_three(b3, i, b)
@@ -368,9 +415,9 @@
     for half in range(2):
         lanes = slice(half * 128, half * 128 + 128)
         chunk = slice(half * 16, half * 16 + 16)
-        own = mbuf[chunk, 1]
-        mult_o[0, :, :, lanes] = own
-        upd_o[0, :, :, lanes] = prev[chunk] * not_first - own - chg[:, :, lanes]
+        earlier = prev[chunk, 0].astype(F32) + prev[chunk, 1].astype(F32)
+        rest_v[0, :, :, lanes] = earlier * not_first - chg[:, :, lanes]
+    outs[2].start()
 
     for copy in halo:
         copy.wait_send()
@@ -384,17 +431,22 @@
 
     @pl.when(core == 0)
     def _():
-        pltpu.make_async_copy(obuf.at[0:3], obuf.at[0:3], bt_s).wait()
+        pltpu.make_async_copy(obuf.at[0], obuf.at[0], bt_s).wait()
         sent = mbuf.at[0 : CHIPS - 1]
         pltpu.make_async_copy(sent, sent, bs).wait()
         pltpu.make_async_copy(sent, sent, bs).wait()
 
+    for out in outs:
+        out.wait()
+
 
 def local(states, increments, w_first, w_mid, w_last, biases, cov_x, cov_y):
-    vmem = pl.BlockSpec(memory_space=pltpu.VMEM)
     anywhere = pl.BlockSpec(memory_space=pl.ANY)
     dma = pltpu.SemaphoreType.DMA
     scratch = [
+        pltpu.VMEM((1, 16, 4, 256), F32),
+        pltpu.VMEM((1, 16, 4, 256), F32),
+        pltpu.VMEM((3, 128), F32),
         pltpu.VMEM((9, 16, 128), BF16),
         pltpu.VMEM((2, 9, 128, 128), BF16),
         pltpu.VMEM((9, 16, 128), BF16),
@@ -423,28 +475,36 @@
         pltpu.VMEM((256, 768), BF16),
         pltpu.VMEM((768, 256), BF16),
         pltpu.VMEM((16, 4, 256), F32),
-        pltpu.VMEM((32, 4, 128), F32),
+        pltpu.VMEM((32, 2, 4, 128), BF16),
         pltpu.VMEM((16, 4, 256), F32),
+        pltpu.VMEM((3, 16, 4, 256), F32),
         pltpu.VMEM((32, 4, 128), F32),
         pltpu.VMEM((TILES, 4, 128), F32),
-        pltpu.VMEM((TILES + 2, 4, 128), F32),
-        pltpu.VMEM((32, 3, 4, 128), F32),
-        dma((5,)), dma((4,)), dma((4,)),
+        pltpu.VMEM((TILES, 4, 4, 128), BF16),
+        pltpu.VMEM((32, 4, 4, 128), BF16),
+        pltpu.VMEM((1, 16, 4, 256), BF16),
+        pltpu.VMEM((1, 16, 4, 256), BF16),
+        pltpu.VMEM((1, 16, 4, 256), F32),
+        dma((3,)), dma((5,)), dma((3,)), pltpu.SemaphoreType.REGULAR((4,)),
+        dma((4,)), dma((4,)),
         dma, dma, dma, dma,
         dma, dma, dma, dma, dma,
         dma, dma, dma, dma, dma,
     ]
-    return pl.pallas_call(
+    high, low, rest = pl.pallas_call(
         kernel,
         out_shape=[
-            jax.ShapeDtypeStruct(states.shape, F32),
+            jax.ShapeDtypeStruct(states.shape, BF16),
+            jax.ShapeDtypeStruct(states.shape, BF16),
             jax.ShapeDtypeStruct(states.shape, F32),
         ],
-        in_specs=[vmem, vmem, anywhere, anywhere, anywhere, vmem, anywhere, anywhere],
-        out_specs=[vmem, vmem],
+        in_specs=[anywhere] * 8,
+        out_specs=[anywhere] * 3,
         scratch_shapes=scratch,
         compiler_params=pltpu.CompilerParams(collective_id=0, has_side_effects=True),
     )(states, increments, w_first, w_mid, w_last, biases, cov_x, cov_y)
+    multiplier = high.astype(F32) + low.astype(F32)
+    return multiplier, rest - multiplier
 
 
 def solution(mesh):

time: 43.5 us -> 39.1 us (0.90)
  Pallas kernels: 40.5 us -> 36.8 us
  local copies, waits for them, and re-layouts: 2.14 us -> 0 us
  other arithmetic: 0 us -> 1.52 us
    pallas_call x1, Pallas kernels: 40.5 us -> 36.8 us  [local(): pl.pallas_call(kernel, out_shape=[jax.ShapeDtypeStruct(states.shape, BF16...]
    unnamed x4 -> x0, local copies, waits for them, and re-layouts: 2.14 us -> none
    sub x0 -> x1, other arithmetic: none -> 1.52 us  [local(): return (multiplier, rest - multiplier)]
where the time goes in v2:
time: 39.1 us; the launch traced here: 38.9 us
  Pallas kernels  36.8 us (94%)
  other arithmetic  1.52 us (4%)
  between operations  0.64 us (2%)
    pallas_call x1, Pallas kernels, local(): pl.pallas_call(kernel, out_shape=[jax.ShapeDtypeStruct(states.shape, BF16...  36.8 us
    sub x1, other arithmetic, local(): return (multiplier, rest - multiplier)  1.52 us

profile of v2, /device:TPU:1, one launch (start us, length us, event | category | flops | bytes accessed | tf_op | source)
XLA Modules:
  0.0 38.9 jit_solution(10662023589783270000)
XLA Ops:
  0.6 36.8 %shard_map.95 = (bf16[1,16,4,256]{3,2,1,0:T(4,128)(2,1)}, bf16[1,16,4,256]{3,2,1,0:T(4,128)(2,1)}, f32[1,16,4,256]{3,2,1,0:T(4,128)}) custom-call(f32[1,16,4,256]{3,2,1,0:T(4,128)} %st_h.1, f32[1,16,4,256]{3,2,1,0:T(4,128)} %inc_h.1, bf16[9,16,128]{2,1,0:T(8,128)(2,1)} %wf_h.1, bf16[2,9,128,128]{3,2,1,0:T(8,128)(2,1)} %wm_h.1, bf16[9,16,128]{2,1,0:T(8,128)(2,1)} %wl_h.1, ...), custom_call_target="tpu_custom_call" | custom-call | tf_op jit(solution)/shard_map/pallas_call | solution.py:494
  37.4 1.5 %fusion = (f32[1,8,8,256]{3,2,1,0:T(8,128)}, f32[1,8,8,256]{3,2,1,0:T(8,128)}) fusion(f32[1,8,8,256]{3,2,1,0:T(8,128)} %bitcast.7, bf16[1,8,8,256]{3,2,1,0:T(8,128)(2,1)} %bitcast.9, bf16[1,8,8,256]{3,2,1,0:T(8,128)(2,1)} %bitcast.8), kind=kLoop, calls=%fused_computation.1 | loop fusion | flops 65536 | bytes 262144 | tf_op jit(solution)/shard_map/sub | solution.py:507

commit v3 on v2

--- a/solution.py
+++ b/solution.py
@@ -110,15 +110,17 @@
     st, inc, bias, wf, wm, wl, cx, cy,
     x, xq, tq, a1, t1, a2, t2, t3, b3, b2, b1, s1, s2, s3,
     w1, wk2, wk3, v4, vk3, vk2, cx3, cy3,
-    nxt, prev, chg, bx, sbuf, rbuf, obuf, mbuf, high_v, low_v, rest_v,
-    insem, wsem, outsem, near, hs, hr, ns, nr, ps, pr, as_, ar, at_s, at_r, al, bs, br, bt_s, bt_r, bl,
+    nxt, prev, chg, bx, sbuf, rbuf, obuf, mbuf,
+    insem, wsem, near, hs, hr, ns, nr, ps, pr, as_, ar, at_s, at_r, al, bs, br, bt_s, bt_r, bl,
 ):
     tm = lax.axis_index("tm")
     me = lax.axis_index("tile")
     chip = lax.div(me, 2)
     core = lax.rem(me, 2)
-    tm_next = lax.rem(tm + 1, WINDOWS)
-    tm_back = lax.rem(tm + WINDOWS - 1, WINDOWS)
+    has_next = tm < WINDOWS - 1
+    has_back = tm > 0
+    tm_next = jnp.minimum(tm + 1, WINDOWS - 1)
+    tm_back = jnp.maximum(tm - 1, 0)
 
     def tile_at(step):
         return lax.rem(me + (step + TILES), TILES)
@@ -128,8 +130,12 @@
         pl.semaphore_signal(
             barrier, inc=1, device_id={"tile": tile_at(step)}, device_id_type=MESH
         )
-    for to in (tm_next, tm_back):
-        pl.semaphore_signal(barrier, inc=1, device_id={"tm": to}, device_id_type=MESH)
+
+    @pl.when(has_next)
+    def _():
+        pl.semaphore_signal(
+            barrier, inc=1, device_id={"tm": tm_next}, device_id_type=MESH
+        )
 
     takes = [
         pltpu.make_async_copy(src, dst, insem.at[n])
@@ -160,7 +166,7 @@
     for r in range(4):
         x[6 + r, 1] = inc[0, :, r, :].astype(BF16)
 
-    pl.semaphore_wait(barrier, 6)
+    pl.semaphore_wait(barrier, jnp.where(has_back, 5, 4))
 
     halo = []
     for n, (step, src, dst) in enumerate(
@@ -182,8 +188,12 @@
     ahead = pltpu.make_async_remote_copy(
         inc.at[0], nxt, ns, nr, device_id={"tm": tm_back}, device_id_type=MESH
     )
-    ahead.start()
     tell(0)
+
+    @pl.when(has_back)
+    def _():
+        ahead.start()
+
 
     def valid(e):
         g = 4 * me - 6 + e
@@ -201,6 +211,8 @@
         put_taps(tq, e, x[e, 1].astype(F32))
     loads[0].wait()
     build_thin(w1, lambda t: wf[t])
+    hear(0)
+    tell(1)
     loads[1].wait()
     build_wide(wk2, lambda t: wm[0, t])
     build_wide(wk3, lambda t: wm[1, t])
@@ -217,20 +229,14 @@
     cy3[256:512] = high
     cy3[512:768] = low
     takes[2].wait()
+    hear(1)
+    tell(2)
     biases = [jnp.concatenate([bias[l : l + 1], bias[l : l + 1]], axis=1) for l in range(3)]
-
-    hear(0)
-    tell(1)
-    for copy in halo[:2]:
-        copy.wait_recv()
 
     def edge_row(e, with_tangent):
         put_taps(xq, e, x[e, 0].astype(F32) * valid(e))
         if with_tangent:
             put_taps(tq, e, x[e, 1].astype(F32) * valid(e))
-
-    for e in (2, 3, 4, 5, 10, 11, 12, 13):
-        edge_row(e, True)
 
     def activation(l, z, e, s_buf, i, out):
         h = jnp.tanh(z + biases[l])
@@ -259,14 +265,18 @@
         if tangent:
             t3[i] = (s * wide_conv(t2, i, wk3)).astype(BF16)
 
-    for i in range(1, 6):
+    layer_one(3, True)
+    for copy in halo[:2]:
+        copy.wait_recv()
+
+    for e in (2, 3, 4, 5, 10, 11, 12, 13):
+        edge_row(e, True)
+    for i in (1, 2, 4, 5):
         layer_one(i, True)
-    hear(1)
-    tell(2)
+    hear(2)
+    tell(3)
     for i in range(1, 5):
         layer_two(i, True)
-    hear(2)
-    tell(3)
     for i in range(1, 4):
         layer_three(i, True)
 
@@ -278,9 +288,15 @@
     for r in range(4):
         chg[:, r, :] = fold_rows(parts, r, False)
 
-    ahead.wait_recv()
-    not_last = jnp.where(tm == WINDOWS - 1, 0.0, 1.0).astype(F32)
-    misfit = nxt[...] * not_last - inc[0] - chg[...]
+    @pl.when(has_next)
+    def _():
+        ahead.wait_recv()
+
+    @pl.when(tm == WINDOWS - 1)
+    def _():
+        nxt[...] = jnp.zeros(nxt.shape, F32)
+
+    misfit = nxt[...] - inc[0] - chg[...]
     high, low = split(misfit.reshape(64, 256))
     smoothed = contract(jnp.concatenate([high, low, high], axis=1), cy3[...])
     for half in range(2):
@@ -373,21 +389,19 @@
     behind = pltpu.make_async_remote_copy(
         mbuf.at[:, 2:4], prev, ps, pr, device_id={"tm": tm_next}, device_id_type=MESH
     )
-    behind.start()
+
+    @pl.when(has_next)
+    def _():
+        behind.start()
+
 
     for half in range(2):
         lanes = slice(half * 128, half * 128 + 128)
         chunk = slice(half * 16, half * 16 + 16)
         for j, slot in enumerate((0, 2, 1)):
             bx[j, :, :, lanes] = mbuf[chunk, slot].astype(F32)
-        high_v[0, :, :, lanes] = mbuf[chunk, 2]
-        low_v[0, :, :, lanes] = mbuf[chunk, 3]
-    outs = [
-        pltpu.make_async_copy(src, dst, outsem.at[n])
-        for n, (src, dst) in enumerate(((high_v, high_o), (low_v, low_o), (rest_v, rest_o)))
-    ]
-    outs[0].start()
-    outs[1].start()
+        high_o[0, :, :, lanes] = mbuf[chunk, 2]
+        low_o[0, :, :, lanes] = mbuf[chunk, 3]
 
     for idx in range(12):
         j, k = idx // 4, idx % 4
@@ -410,19 +424,31 @@
     for r in range(4):
         chg[:, r, :] = fold_rows(parts, r, True)
 
-    behind.wait_recv()
-    not_first = jnp.where(tm == 0, 0.0, 1.0).astype(F32)
+    @pl.when(has_back)
+    def _():
+        behind.wait_recv()
+
+    @pl.when(tm == 0)
+    def _():
+        prev[...] = jnp.zeros(prev.shape, BF16)
+
     for half in range(2):
         lanes = slice(half * 128, half * 128 + 128)
         chunk = slice(half * 16, half * 16 + 16)
         earlier = prev[chunk, 0].astype(F32) + prev[chunk, 1].astype(F32)
-        rest_v[0, :, :, lanes] = earlier * not_first - chg[:, :, lanes]
-    outs[2].start()
+        rest_o[0, :, :, lanes] = earlier - chg[:, :, lanes]
 
     for copy in halo:
         copy.wait_send()
-    ahead.wait_send()
-    behind.wait_send()
+
+    @pl.when(has_back)
+    def _():
+        ahead.wait_send()
+
+    @pl.when(has_next)
+    def _():
+        behind.wait_send()
+
     pltpu.make_async_copy(sbuf.at[0 : CHIPS - 1], sbuf.at[0 : CHIPS - 1], as_).wait()
 
     @pl.when(core == 1)
@@ -435,9 +461,6 @@
         sent = mbuf.at[0 : CHIPS - 1]
         pltpu.make_async_copy(sent, sent, bs).wait()
         pltpu.make_async_copy(sent, sent, bs).wait()
-
-    for out in outs:
-        out.wait()
 
 
 def local(states, increments, w_first, w_mid, w_last, biases, cov_x, cov_y):
@@ -482,10 +505,7 @@
         pltpu.VMEM((TILES, 4, 128), F32),
         pltpu.VMEM((TILES, 4, 4, 128), BF16),
         pltpu.VMEM((32, 4, 4, 128), BF16),
-        pltpu.VMEM((1, 16, 4, 256), BF16),
-        pltpu.VMEM((1, 16, 4, 256), BF16),
-        pltpu.VMEM((1, 16, 4, 256), F32),
-        dma((3,)), dma((5,)), dma((3,)), pltpu.SemaphoreType.REGULAR((4,)),
+        dma((3,)), dma((5,)), pltpu.SemaphoreType.REGULAR((4,)),
         dma((4,)), dma((4,)),
         dma, dma, dma, dma,
         dma, dma, dma, dma, dma,
@@ -494,12 +514,12 @@
     high, low, rest = pl.pallas_call(
         kernel,
         out_shape=[
-            jax.ShapeDtypeStruct(states.shape, BF16),
-            jax.ShapeDtypeStruct(states.shape, BF16),
-            jax.ShapeDtypeStruct(states.shape, F32),
+            pltpu.VMEM(states.shape, BF16),
+            pltpu.VMEM(states.shape, BF16),
+            pltpu.VMEM(states.shape, F32),
         ],
         in_specs=[anywhere] * 8,
-        out_specs=[anywhere] * 3,
+        out_specs=[pl.BlockSpec(memory_space=pltpu.VMEM)] * 3,
         scratch_shapes=scratch,
         compiler_params=pltpu.CompilerParams(collective_id=0, has_side_effects=True),
     )(states, increments, w_first, w_mid, w_last, biases, cov_x, cov_y)

time: 39.1 us -> 35.9 us (0.918)
  Pallas kernels: 36.8 us -> 34.5 us
  other arithmetic: 1.52 us -> 0.66 us
    pallas_call x1, Pallas kernels: 36.8 us -> 34.5 us  [local(): pl.pallas_call(kernel, out_shape=[pltpu.VMEM(states.shape, BF16), pltpu.V...]
    sub x1, other arithmetic: 1.52 us -> 0.66 us  [local(): return (multiplier, rest - multiplier)]
where the time goes in v3:
time: 35.9 us; the launch traced here: 35.8 us
  Pallas kernels  34.5 us (96%)
  other arithmetic  0.66 us (2%)
  between operations  0.64 us (2%)
    pallas_call x1, Pallas kernels, local(): pl.pallas_call(kernel, out_shape=[pltpu.VMEM(states.shape, BF16), pltpu.V...  34.5 us

profile of v3, /device:TPU:1, one launch (start us, length us, event | category | flops | bytes accessed | tf_op | source)
XLA Modules:
  0.0 35.8 jit_solution(9903624967624659198)
XLA Ops:
  0.6 34.5 %shard_map.95 = (bf16[1,16,4,256]{3,2,1,0:T(4,128)(2,1)S(1)}, bf16[1,16,4,256]{3,2,1,0:T(4,128)(2,1)S(1)}, f32[1,16,4,256]{3,2,1,0:T(4,128)S(1)}) custom-call(f32[1,16,4,256]{3,2,1,0:T(4,128)} %st_h.1, f32[1,16,4,256]{3,2,1,0:T(4,128)} %inc_h.1, bf16[9,16,128]{2,1,0:T(8,128)(2,1)} %wf_h.1, bf16[2,9,128,128]{3,2,1,0:T(8,128)(2,1)} %wm_h.1, ...), custom_call_target="tpu_custom_call" | custom-call | tf_op jit(solution)/shard_map/pallas_call | solution.py:514
  35.1 0.7 %fusion = (f32[1,8,8,256]{3,2,1,0:T(8,128)}, f32[1,8,8,256]{3,2,1,0:T(8,128)}) fusion(f32[1,8,8,256]{3,2,1,0:T(8,128)S(1)} %bitcast.5, bf16[1,8,8,256]{3,2,1,0:T(8,128)(2,1)S(1)} %bitcast.7, bf16[1,8,8,256]{3,2,1,0:T(8,128)(2,1)S(1)} %bitcast.6), kind=kLoop, calls=%fused_computation.1 | loop fusion | flops 65536 | bytes 262144 | tf_op jit(solution)/shard_map/sub | solution.py:527

commit v4 on v3

--- a/solution.py
+++ b/solution.py
@@ -126,10 +126,13 @@
         return lax.rem(me + (step + TILES), TILES)
 
     barrier = pltpu.get_barrier_semaphore()
-    for step in (1, -1, 2, -2):
-        pl.semaphore_signal(
-            barrier, inc=1, device_id={"tile": tile_at(step)}, device_id_type=MESH
-        )
+    def greet(to):
+        pl.semaphore_signal(barrier, inc=1, device_id={"tile": to}, device_id_type=MESH)
+
+    for step in (1, -1, 2, -2, 8, -8, 16, -16):
+        greet(tile_at(step))
+    for step in range(1, 8):
+        greet(lax.div(me, 8) * 8 + lax.rem(me + step, 8))
 
     @pl.when(has_next)
     def _():
@@ -151,13 +154,13 @@
         load.start()
 
     def tell(n):
-        for step in (2 << n, -(2 << n)):
+        for step in (8, -8, 16, -16):
             pl.semaphore_signal(
                 near.at[n], inc=1, device_id={"tile": tile_at(step)}, device_id_type=MESH
             )
 
     def hear(n):
-        pl.semaphore_wait(near.at[n], 2)
+        pl.semaphore_wait(near.at[n], 4)
 
     takes[0].wait()
     for r in range(4):
@@ -166,7 +169,7 @@
     for r in range(4):
         x[6 + r, 1] = inc[0, :, r, :].astype(BF16)
 
-    pl.semaphore_wait(barrier, jnp.where(has_back, 5, 4))
+    pl.semaphore_wait(barrier, jnp.where(has_back, 16, 15))
 
     halo = []
     for n, (step, src, dst) in enumerate(
@@ -229,8 +232,6 @@
     cy3[256:512] = high
     cy3[512:768] = low
     takes[2].wait()
-    hear(1)
-    tell(2)
     biases = [jnp.concatenate([bias[l : l + 1], bias[l : l + 1]], axis=1) for l in range(3)]
 
     def edge_row(e, with_tangent):
@@ -273,8 +274,6 @@
         edge_row(e, True)
     for i in (1, 2, 4, 5):
         layer_one(i, True)
-    hear(2)
-    tell(3)
     for i in range(1, 5):
         layer_two(i, True)
     for i in range(1, 4):
@@ -304,7 +303,7 @@
             16, 4, 128
         )
 
-    hear(3)
+    hear(1)
 
     def chip_at(dz, dx):
         return lax.rem(lax.div(chip, 4) + dz, 8) * 4 + lax.rem(chip + dx, 4)
@@ -505,7 +504,7 @@
         pltpu.VMEM((TILES, 4, 128), F32),
         pltpu.VMEM((TILES, 4, 4, 128), BF16),
         pltpu.VMEM((32, 4, 4, 128), BF16),
-        dma((3,)), dma((5,)), pltpu.SemaphoreType.REGULAR((4,)),
+        dma((3,)), dma((5,)), pltpu.SemaphoreType.REGULAR((2,)),
         dma((4,)), dma((4,)),
         dma, dma, dma, dma,
         dma, dma, dma, dma, dma,

time: 35.9 us -> 33.1 us (0.922)
  Pallas kernels: 34.5 us -> 31.7 us
    pallas_call x1, Pallas kernels: 34.5 us -> 31.7 us  [local(): pl.pallas_call(kernel, out_shape=[pltpu.VMEM(states.shape, BF16), pltpu.V...]
where the time goes in v4:
time: 33.1 us; the launch traced here: 33 us
  Pallas kernels  31.7 us (96%)
  other arithmetic  0.66 us (2%)
  between operations  0.64 us (2%)
    pallas_call x1, Pallas kernels, local(): pl.pallas_call(kernel, out_shape=[pltpu.VMEM(states.shape, BF16), pltpu.V...  31.7 us
    sub x1, other arithmetic, local(): return (multiplier, rest - multiplier)  0.66 us

profile of v4, /device:TPU:1, one launch (start us, length us, event | category | flops | bytes accessed | tf_op | source)
XLA Modules:
  0.0 33.0 jit_solution(11819163879514075209)
XLA Ops:
  0.6 31.7 %shard_map.95 = (bf16[1,16,4,256]{3,2,1,0:T(4,128)(2,1)S(1)}, bf16[1,16,4,256]{3,2,1,0:T(4,128)(2,1)S(1)}, f32[1,16,4,256]{3,2,1,0:T(4,128)S(1)}) custom-call(f32[1,16,4,256]{3,2,1,0:T(4,128)} %st_h.1, f32[1,16,4,256]{3,2,1,0:T(4,128)} %inc_h.1, bf16[9,16,128]{2,1,0:T(8,128)(2,1)} %wf_h.1, bf16[2,9,128,128]{3,2,1,0:T(8,128)(2,1)} %wm_h.1, ...), custom_call_target="tpu_custom_call" | custom-call | tf_op jit(solution)/shard_map/pallas_call | solution.py:513
  32.3 0.7 %fusion = (f32[1,8,8,256]{3,2,1,0:T(8,128)}, f32[1,8,8,256]{3,2,1,0:T(8,128)}) fusion(f32[1,8,8,256]{3,2,1,0:T(8,128)S(1)} %bitcast.5, bf16[1,8,8,256]{3,2,1,0:T(8,128)(2,1)S(1)} %bitcast.7, bf16[1,8,8,256]{3,2,1,0:T(8,128)(2,1)S(1)} %bitcast.6), kind=kLoop, calls=%fused_computation.1 | loop fusion | flops 65536 | bytes 262144 | tf_op jit(solution)/shard_map/sub | solution.py:526

commit v5 on v4

--- a/solution.py
+++ b/solution.py
@@ -15,6 +15,7 @@
     ((z, x) for z in range(8) for x in range(4) if z or x),
     key=lambda s: -(min(s[0], 8 - s[0]) + min(s[1], 4 - s[1])),
 )
+EARLY_FIRST = (0, 1, 2, 3, 7, 4, 6, 5)
 
 
 def contract(a, b, dims=((1,), (0,))):
@@ -216,21 +217,6 @@
     build_thin(w1, lambda t: wf[t])
     hear(0)
     tell(1)
-    loads[1].wait()
-    build_wide(wk2, lambda t: wm[0, t])
-    build_wide(wk3, lambda t: wm[1, t])
-    loads[2].wait()
-    build_thin(v4, lambda t: wl[8 - t])
-    loads[3].wait()
-    high, low = split(cx[...])
-    cx3[:, 0:256] = high
-    cx3[:, 256:512] = high
-    cx3[:, 512:768] = low
-    loads[4].wait()
-    high, low = split(cy[...])
-    cy3[0:256] = high
-    cy3[256:512] = high
-    cy3[512:768] = low
     takes[2].wait()
     biases = [jnp.concatenate([bias[l : l + 1], bias[l : l + 1]], axis=1) for l in range(3)]
 
@@ -267,17 +253,52 @@
             t3[i] = (s * wide_conv(t2, i, wk3)).astype(BF16)
 
     layer_one(3, True)
-    for copy in halo[:2]:
-        copy.wait_recv()
-
-    for e in (2, 3, 4, 5, 10, 11, 12, 13):
-        edge_row(e, True)
-    for i in (1, 2, 4, 5):
-        layer_one(i, True)
-    for i in range(1, 5):
-        layer_two(i, True)
-    for i in range(1, 4):
-        layer_three(i, True)
+    loads[1].wait()
+    build_wide(wk2, lambda t: wm[0, t])
+
+    def side(upper):
+        halo[1 if upper else 0].wait_recv()
+        for e in (10, 11, 12, 13) if upper else (5, 4, 3, 2):
+            edge_row(e, True)
+        for i in (4, 5) if upper else (2, 1):
+            layer_one(i, True)
+
+    def near_side(upper):
+        side(upper)
+        for i in (3, 4) if upper else (2, 1):
+            layer_two(i, True)
+        build_wide(wk3, lambda t: wm[1, t])
+        layer_three(3 if upper else 1, True)
+
+    def far_side(upper):
+        side(upper)
+        for i in (3, 4) if upper else (2, 1):
+            layer_two(i, True)
+        for i in (2, 3) if upper else (2, 1):
+            layer_three(i, True)
+
+    @pl.when(core == 0)
+    def _():
+        near_side(True)
+
+    @pl.when(core == 1)
+    def _():
+        near_side(False)
+
+    loads[2].wait()
+    loads[4].wait()
+    high, low = split(cy[...])
+    cy3[0:256] = high
+    cy3[256:512] = high
+    cy3[512:768] = low
+
+    @pl.when(core == 0)
+    def _():
+        far_side(False)
+
+    @pl.when(core == 1)
+    def _():
+        far_side(True)
 
     last = wl[...].reshape(144, 128)
     parts = []
@@ -325,6 +346,12 @@
     @pl.when(core == 1)
     def _():
         out_chunk(chip, at_s, at_r).start()
+
+    loads[3].wait()
+    high, low = split(cx[...])
+    cx3[:, 0:256] = high
+    cx3[:, 256:512] = high
+    cx3[:, 512:768] = low
 
     for copy in halo[2:]:
         copy.wait_recv()
@@ -336,6 +363,7 @@
         layer_two(i, False)
     for i in (0, 4):
         layer_three(i, False)
+    build_thin(v4, lambda t: wl[8 - t])
     build_wide(vk3, lambda t: wm[1, 8 - t].T)
     build_wide(vk2, lambda t: wm[0, 8 - t].T)
 
@@ -367,10 +395,15 @@
                 device_id={"tile": d}, device_id_type=MESH,
             )
 
-        for dz, dx in FAR_FIRST:
-            c = chip_at(dz, dx)
-            for half in range(2):
-                back_chunk(2 * c + half, bs, br).start()
+        for z in EARLY_FIRST:
+            for dx in range(4):
+                c = z * 4 + lax.rem(chip + dx, 4)
+
+                @pl.when(c != chip)
+                def _():
+                    for half in range(2):
+                        back_chunk(2 * c + half, bs, br).start()
+
         back_chunk(me + 1, bt_s, bt_r).start()
         own_back = pltpu.make_async_copy(obuf.at[me], mbuf.at[chip], bl)
         own_back.start()

time: 33.1 us -> 32.4 us (0.979)
  Pallas kernels: 31.7 us -> 31 us
    pallas_call x1, Pallas kernels: 31.7 us -> 31 us  [local(): pl.pallas_call(kernel, out_shape=[pltpu.VMEM(states.shape, BF16), pltpu.V...]
where the time goes in v5:
time: 32.4 us; the launch traced here: 32.3 us
  Pallas kernels  31 us (96%)
  other arithmetic  0.66 us (2%)
  between operations  0.64 us (2%)
    pallas_call x1, Pallas kernels, local(): pl.pallas_call(kernel, out_shape=[pltpu.VMEM(states.shape, BF16), pltpu.V...  31 us
    sub x1, other arithmetic, local(): return (multiplier, rest - multiplier)  0.66 us

profile of v5, /device:TPU:1, one launch (start us, length us, event | category | flops | bytes accessed | tf_op | source)
XLA Modules:
  0.0 32.3 jit_solution(12462182634744394452)
XLA Ops:
  0.6 31.0 %shard_map.95 = (bf16[1,16,4,256]{3,2,1,0:T(4,128)(2,1)S(1)}, bf16[1,16,4,256]{3,2,1,0:T(4,128)(2,1)S(1)}, f32[1,16,4,256]{3,2,1,0:T(4,128)S(1)}) custom-call(f32[1,16,4,256]{3,2,1,0:T(4,128)} %st_h.1, f32[1,16,4,256]{3,2,1,0:T(4,128)} %inc_h.1, bf16[9,16,128]{2,1,0:T(8,128)(2,1)} %wf_h.1, bf16[2,9,128,128]{3,2,1,0:T(8,128)(2,1)} %wm_h.1, ...), custom_call_target="tpu_custom_call" | custom-call | tf_op jit(solution)/shard_map/pallas_call | solution.py:546
  31.6 0.7 %fusion = (f32[1,8,8,256]{3,2,1,0:T(8,128)}, f32[1,8,8,256]{3,2,1,0:T(8,128)}) fusion(f32[1,8,8,256]{3,2,1,0:T(8,128)S(1)} %bitcast.5, bf16[1,8,8,256]{3,2,1,0:T(8,128)(2,1)S(1)} %bitcast.7, bf16[1,8,8,256]{3,2,1,0:T(8,128)(2,1)S(1)} %bitcast.6), kind=kLoop, calls=%fused_computation.1 | loop fusion | flops 65536 | bytes 262144 | tf_op jit(solution)/shard_map/sub | solution.py:559

commit v6 on v5

--- a/solution.py
+++ b/solution.py
@@ -187,7 +187,7 @@
                 device_id={"tile": lax.rem(me + step, TILES)}, device_id_type=MESH,
             )
         )
-    for copy in halo:
+    for copy in halo[:2]:
         copy.start()
     ahead = pltpu.make_async_remote_copy(
         inc.at[0], nxt, ns, nr, device_id={"tm": tm_back}, device_id_type=MESH
@@ -285,6 +285,8 @@
     def _():
         near_side(False)
 
+    for copy in halo[2:]:
+        copy.start()
     loads[2].wait()
     loads[4].wait()
     high, low = split(cy[...])

time: 32.4 us -> 32.4 us (level)
  no operation moved by 1% of the time
where the time goes in v6:
time: 32.4 us; the launch traced here: 32.3 us
  Pallas kernels  31 us (96%)
  other arithmetic  0.66 us (2%)
  between operations  0.64 us (2%)
    pallas_call x1, Pallas kernels, local(): pl.pallas_call(kernel, out_shape=[pltpu.VMEM(states.shape, BF16), pltpu.V...  31 us
    sub x1, other arithmetic, local(): return (multiplier, rest - multiplier)  0.66 us

profile of v6, /device:TPU:1, one launch (start us, length us, event | category | flops | bytes accessed | tf_op | source)
XLA Modules:
  0.0 32.3 jit_solution(9752528170106599635)
XLA Ops:
  0.6 31.0 %shard_map.95 = (bf16[1,16,4,256]{3,2,1,0:T(4,128)(2,1)S(1)}, bf16[1,16,4,256]{3,2,1,0:T(4,128)(2,1)S(1)}, f32[1,16,4,256]{3,2,1,0:T(4,128)S(1)}) custom-call(f32[1,16,4,256]{3,2,1,0:T(4,128)} %st_h.1, f32[1,16,4,256]{3,2,1,0:T(4,128)} %inc_h.1, bf16[9,16,128]{2,1,0:T(8,128)(2,1)} %wf_h.1, bf16[2,9,128,128]{3,2,1,0:T(8,128)(2,1)} %wm_h.1, ...), custom_call_target="tpu_custom_call" | custom-call | tf_op jit(solution)/shard_map/pallas_call | solution.py:548
  31.7 0.7 %fusion = (f32[1,8,8,256]{3,2,1,0:T(8,128)}, f32[1,8,8,256]{3,2,1,0:T(8,128)}) fusion(f32[1,8,8,256]{3,2,1,0:T(8,128)S(1)} %bitcast.5, bf16[1,8,8,256]{3,2,1,0:T(8,128)(2,1)S(1)} %bitcast.7, bf16[1,8,8,256]{3,2,1,0:T(8,128)(2,1)S(1)} %bitcast.6), kind=kLoop, calls=%fused_computation.1 | loop fusion | flops 65536 | bytes 262144 | tf_op jit(solution)/shard_map/sub | solution.py:561
